TPU v7x, 256 devices: a whole 4x4x8 slice. The times are simulated.
256 devices in a mesh: row: 16 (over x, z_lo), col: 16 (over z_hi, y, core).
Axes of the slice: x: 4, y: 4, z: 8 (z_hi: 2, z_lo: 4; z = z_hi * 4 + z_lo), core: 2. Of those that a mesh axis runs over, the one named last changes fastest.
Arguments:
- factors: bfloat16 [32768, 256], P(('row', 'col')), may hold values from -1.5 to 1.5
- cores: bfloat16 [8, 256, 256], replicated, may hold values from -0.375 to 0.375
- tiles: bfloat16 [8192, 256, 256], P(('row', 'col')), may hold values from -6 to 6
- tile_coords: int32 [8192, 3], P(('row', 'col')), may hold values from 0 to 7, as said below
- tile_counts: int32 [256], P(('row', 'col')), may hold values from 1 to 32, as said below
Outputs:
- gradient: float32 [32768, 256], P(('row', 'col'))
Inputs may be any that keep to these rules, and one draw needn't show every extreme that they name: `tile_coords`: column 0 is a relation below 8, column 1 below 8, column 2 below 8; within one device no two slots have the same three coordinates. `tile_counts`: some device has all 32 slots live.
All inputs are finite; a program needn't handle non-finite values.
Results may differ from a plain program's by a relative error of at most 0.0011.
Values may be sent and summed in bfloat16 or wider, within the bound.
A program may use at most 128 MiB of HBM per device.

v0:
```python
import jax
import jax.numpy as jnp
from jax import lax
from jax.sharding import PartitionSpec as P

weight_decay = 1.0


def broadcast(value, axis, source):
    kept = jnp.where(lax.axis_index(axis) == source, value, 0).astype(value.dtype)
    return lax.psum(kept, axis)


def local(factors, cores, tiles, tile_coords, tile_counts):
    n_row = lax.axis_size("row")
    n_col = lax.axis_size("col")
    row_ratio = n_row // n_col
    shard_rows, rank_width = factors.shape
    tile_size = tiles.shape[1]
    relations = cores.shape[0]
    src_rows = shard_rows * n_col
    tgt_rows = src_rows * row_ratio
    src_blocks = src_rows // tile_size
    tgt_blocks = tgt_rows // tile_size
    row_pos = lax.axis_index("row")
    col_pos = lax.axis_index("col")
    source = lax.all_gather(factors, "col", axis=0, tiled=True)
    received = broadcast(source, "row", col_pos * row_ratio + 0)
    left_core = jnp.einsum("nr,krs->kns", source, cores, preferred_element_type=jnp.float32).astype(
        jnp.bfloat16
    )
    left_core = left_core.reshape(relations, src_blocks, tile_size, rank_width)
    right_core = jnp.einsum(
        "nr,ksr->kns", received, cores, preferred_element_type=jnp.float32
    ).astype(jnp.bfloat16)
    right_core = right_core.reshape(relations, tgt_blocks, tile_size, rank_width)
    tgt_factor = received.reshape(tgt_blocks, tile_size, rank_width)
    live_count = tile_counts[0]

    def group_pass(group, carry):
        grad_src, grad_tgt = carry
        start = group * 8
        coords = lax.dynamic_slice_in_dim(tile_coords, start, 8, 0)
        values = lax.dynamic_slice_in_dim(tiles, start, 8, 0)
        is_live = start + jnp.arange(8, dtype=jnp.int32) < live_count
        relation = coords[:, 0]
        src_index = coords[:, 1]
        tgt_index = coords[:, 2]
        left = left_core[relation, src_index]
        right = tgt_factor[tgt_index]
        right_rel = right_core[relation, tgt_index]
        predicted = jnp.einsum("gtr,gur->gtu", left, right, preferred_element_type=jnp.float32)
        resid = jnp.where(
            is_live[:, None, None], values.astype(jnp.float32) - predicted, 0.0
        ).astype(jnp.bfloat16)
        src_grad = jnp.einsum("gtu,gur->gtr", resid, right_rel, preferred_element_type=jnp.float32)
        tgt_grad = jnp.einsum("gtu,gtr->gur", resid, left, preferred_element_type=jnp.float32)
        return (grad_src.at[src_index].add(src_grad), grad_tgt.at[tgt_index].add(tgt_grad))

    start_grads = (
        jnp.zeros((src_blocks, tile_size, rank_width), jnp.float32),
        jnp.zeros((tgt_blocks, tile_size, rank_width), jnp.float32),
    )
    grad_src, grad_tgt = lax.fori_loop(0, (live_count + 7) // 8, group_pass, start_grads)
    grad_src = grad_src.reshape(src_rows, rank_width)
    grad_tgt = grad_tgt.reshape(tgt_rows, rank_width)
    tgt_total = lax.psum(grad_tgt, "row")
    summed = lax.psum_scatter(grad_src, "col", scatter_dimension=0, tiled=True)
    relay_block = broadcast(tgt_total, "col", row_pos // row_ratio)
    relay_part = lax.dynamic_slice_in_dim(
        relay_block, (row_pos % row_ratio * n_col + col_pos) * shard_rows, shard_rows, 0
    )
    summed = summed + relay_part
    return weight_decay * factors.astype(jnp.float32) - summed / tile_size


def solution(mesh):
    in_specs = (
        P(("row", "col"), None),
        P(),
        P(("row", "col"), None, None),
        P(("row", "col"), None),
        P(("row", "col")),
    )
    out_specs = P(("row", "col"), None)
    return jax.shard_map(local, mesh=mesh, in_specs=in_specs, out_specs=out_specs, check_vma=False)
```

profile of v0, /device:TPU:1, one launch (start us, length us, event | category | flops | bytes accessed | tf_op | source)
XLA Modules:
  0.0 805.9 jit_solution(2866157427274746892)
XLA Ops:
  7.3 62.5 %all-gather.2.cloned.1.call-done = bf16[2048,256]{1,0:T(8,128)(2,1)} async-done(((bf16[128,256]{1,0:T(8,128)(2,1)}), bf16[2048,256]{1,0:T(8,128)(2,1)}) %all-gather.2.cloned.1.call-update) | async-done | bytes 1048592 | tf_op jit(solution)/shard_map/all_gather | solution.py:27
  71.7 5.6 convert_bitcast_fusion
  77.3 11.4 %copy.11 = bf16[8,2048,256]{2,1,0:T(8,128)(2,1)} copy(bf16[8,2048,256]{1,2,0:T(8,128)(2,1)} %convert_bitcast_fusion) | data formatting | bytes 16777216 | tf_op jit(solution)/shard_map/while | solution.py:64
  88.7 135.2 %all-reduce.4.cloned.1.call-done = bf16[2048,256]{1,0:T(8,128)(2,1)} async-done(((bf16[2048,256]{1,0:T(8,128)(2,1)}), bf16[2048,256]{1,0:T(8,128)(2,1)}) %all-reduce.4.cloned.1.call-update) | async-done | bytes 1048592 | tf_op jit(solution)/shard_map/psum | solution.py:11
  223.9 6.8 convolution_convert_fusion
  233.7 82.3 %while.12 = (s32[]{:T(128)}, f32[8,256,256]{2,1,0:T(8,128)}, f32[8,256,256]{2,1,0:T(8,128)}, s32[]{:T(128)}, s32[32,3]{0,1:T(4,128)S(1)}, /*index=5*/s32[]{:T(12...) while((s32[]{:T(128)}, f32[8,256,256]{2,1,0:T(8,128)}, ...), condition=%wide.region_4.5_spmd, body=%wide.region_1.4_spmd.sunk | while | flops 808453248 | bytes 39850920 | solution.py:64
  234.4 1.8 gather_fusion.1
  236.3 4.0 gather_fusion
  241.3 1.7 select_convert_fusion.2
  244.0 1.7 fusion.31
  245.7 4.1 scatter_fusion.1
  249.9 5.0 gather_fusion.2
  254.8 2.0 fusion.30
  256.8 4.2 scatter_fusion
  261.8 1.8 gather_fusion.1
  263.7 4.0 gather_fusion
  268.7 1.7 select_convert_fusion.2
  271.4 1.7 fusion.31
  273.1 4.2 scatter_fusion.1
  277.3 5.0 gather_fusion.2
  282.3 2.0 fusion.30
  284.3 4.3 scatter_fusion
  289.3 1.8 gather_fusion.1
  291.2 4.0 gather_fusion
  298.9 1.7 fusion.31
  300.6 4.2 scatter_fusion.1
  304.8 5.0 gather_fusion.2
  309.8 2.0 fusion.30
  311.7 4.2 scatter_fusion
  316.6 199.1 %all-reduce.6.cloned.1.call-done = f32[2048,256]{1,0:T(8,128)} async-done(((f32[2048,256]{1,0:T(8,128)}), f32[2048,256]{1,0:T(8,128)}) %all-reduce.6.cloned.1.call-update) | async-done | bytes 2097168 | tf_op jit(solution)/shard_map/psum | solution.py:67
  517.2 95.2 %reduce-scatter.2.cloned.1.call-done = f32[128,256]{1,0:T(8,128)} async-done(((f32[2048,256]{1,0:T(8,128)}), f32[128,256]{1,0:T(8,128)}) %reduce-scatter.2.cloned.1.call-update) | async-done | bytes 131088 | tf_op jit(solution)/shard_map/reduce_scatter | solution.py:68
  612.4 185.3 %all-reduce.8.cloned.1.call-done = f32[2048,256]{1,0:T(8,128)} async-done(((f32[2048,256]{1,0:T(8,128)}), f32[2048,256]{1,0:T(8,128)}) %all-reduce.8.cloned.1.call-update) | async-done | bytes 2097168 | tf_op jit(solution)/shard_map/psum | solution.py:11
  (48 shorter events, 18.4 us)
Async XLA Ops:
  6.5 65.1 %copy-start = (bf16[8,256,256]{2,1,0:T(8,128)(2,1)S(1)}, bf16[8,256,256]{2,1,0:T(8,128)(2,1)}, u32[]{:S(2)}) copy-start(bf16[8,256,256]{2,1,0:T(8,128)(2,1)} %param.8) | copy-start | bytes 3145732
  6.5 63.3 %all-gather.2.cloned.1.call-start = ((), (), s32[]{:S(2)}) async-start(), calls=%async_computation.1 | async-start | bytes 1114112 | tf_op jit(solution)/shard_map/all_gather | solution.py:27
  7.3 216.6 %all-reduce.4.cloned.1.call-start = ((), (), s32[]{:S(2)}) async-start(), calls=%async_computation.2 | async-start | bytes 2097152 | tf_op jit(solution)/shard_map/psum | solution.py:11
  69.8 1.8 copy-start.3
  70.9 444.8 %all-reduce.6.cloned.1.call-start = ((), (), s32[]{:S(2)}) async-start(), calls=%async_computation.4 | async-start | bytes 4194304 | tf_op jit(solution)/shard_map/psum | solution.py:67
  230.7 3.0 copy-start.5
  240.3 1.0 copy-start.1
  243.0 1.0 copy-start.2
  267.7 1.0 copy-start.1
  270.4 1.0 copy-start.2
  295.2 1.0 copy-start.1
  297.9 1.0 copy-start.2
  316.0 296.5 %reduce-scatter.2.cloned.1.call-start = ((), (), s32[]{:S(2)}) async-start(), calls=%async_computation.3 | async-start | bytes 2228224 | tf_op jit(solution)/shard_map/reduce_scatter | solution.py:68
  316.5 481.2 %all-reduce.8.cloned.1.call-start = ((), (), s32[]{:S(2)}) async-start(), calls=%async_computation.5 | async-start | bytes 4194304 | tf_op jit(solution)/shard_map/psum | solution.py:11
  517.2 280.6 %copy-start.4 = (bf16[128,256]{1,0:T(8,128)(2,1)S(1)}, bf16[128,256]{1,0:T(8,128)(2,1)}, u32[]{:S(2)}) copy-start(bf16[128,256]{1,0:T(8,128)(2,1)} %param.7) | copy-start | bytes 196612
Sparse Core Ops, SparseCore 0:
  10.1 59.7 all-gather.1
  72.5 151.3 all-reduce.3
  316.1 199.6 all-reduce.5
  519.8 92.5 reduce-scatter.1
  614.9 182.7 all-reduce.7
where the time goes:
time: 807 us; the launch traced here: 806 us
  waiting for transfers between devices  679 us (84%)
  local copies, waits for them, and re-layouts  53 us (7%)
  other arithmetic  31.4 us (4%)
  matrix products  28.6 us (4%)
  between operations  13.8 us (2%)
    psum x2, waiting for transfers between devices, broadcast(): return lax.psum(kept, axis)  320 us
    psum x1, waiting for transfers between devices, local(): tgt_total = lax.psum(grad_tgt, 'row')  199 us
    reduce_scatter x1, waiting for transfers between devices, local(): summed = lax.psum_scatter(grad_src, 'col', scatter_dimension=0, tiled=True)  95.2 us
    all_gather x1, waiting for transfers between devices, local(): source = lax.all_gather(factors, 'col', axis=0, tiled=True)  62.5 us
  transfers between devices with their start and end apart: 5, of which 5 were waited for; matrix products, arithmetic and copies ran while one was open for 2% of the time, Pallas kernels for 0%

commit v1 on v0

--- a/solution.py
+++ b/solution.py
@@ -8,7 +8,7 @@
 
 def broadcast(value, axis, source):
     kept = jnp.where(lax.axis_index(axis) == source, value, 0).astype(value.dtype)
-    return lax.psum(kept, axis)
+    return jnp.sum(lax.all_gather(kept, axis), axis=0)
 
 
 def local(factors, cores, tiles, tile_coords, tile_counts):

time: 807 us -> 1130 us (1.40)
  waiting for transfers between devices: 679 us -> 978 us
  other arithmetic: 31.4 us -> 53.5 us
    all_gather x0 -> x2, waiting for transfers between devices: none -> 650 us  [broadcast(): return jnp.sum(lax.all_gather(kept, axis), axis=0)]
    psum x2 -> x0, waiting for transfers between devices: 320 us -> none  [broadcast(): return lax.psum(kept, axis)]
    reduce_scatter x1, waiting for transfers between devices: 95.2 us -> 71.4 us  [local(): summed = lax.psum_scatter(grad_src, 'col', scatter_dimension=0, tiled=True)]
    reduce_sum x0 -> x2, other arithmetic: none -> 22.2 us  [broadcast(): return jnp.sum(lax.all_gather(kept, axis), axis=0)]
  transfers between devices with their start and end apart: 5 -> 5, of which waited for: 5 -> 5; matrix products, arithmetic and copies ran while one was open for 2% -> 3% of each run, Pallas kernels for 0% -> 0%
where the time goes in v1:
time: 1130 us; the launch traced here: 1120 us
  waiting for transfers between devices  978 us (87%)
  other arithmetic  53.5 us (5%)
  local copies, waits for them, and re-layouts  47.1 us (4%)
  matrix products  31.6 us (3%)
  between operations  13.9 us (1%)
    all_gather x2, waiting for transfers between devices, broadcast(): return jnp.sum(lax.all_gather(kept, axis), axis=0)  650 us
    psum x1, waiting for transfers between devices, local(): tgt_total = lax.psum(grad_tgt, 'row')  193 us
    reduce_scatter x1, waiting for transfers between devices, local(): summed = lax.psum_scatter(grad_src, 'col', scatter_dimension=0, tiled=True)  71.4 us
    all_gather x1, waiting for transfers between devices, local(): source = lax.all_gather(factors, 'col', axis=0, tiled=True)  62.5 us
  transfers between devices with their start and end apart: 5, of which 5 were waited for; matrix products, arithmetic and copies ran while one was open for 3% of the time, Pallas kernels for 0%

profile of v1, /device:TPU:1, one launch (start us, length us, event | category | flops | bytes accessed | tf_op | source)
XLA Modules:
  0.0 1123.9 jit_solution(10669330868088825802)
XLA Ops:
  7.3 62.5 %all-gather.6.cloned.1.call-done = bf16[2048,256]{1,0:T(8,128)(2,1)} async-done(((bf16[128,256]{1,0:T(8,128)(2,1)}), bf16[2048,256]{1,0:T(8,128)(2,1)}) %all-gather.6.cloned.1.call-update) | async-done | bytes 1048592 | tf_op jit(solution)/shard_map/all_gather | solution.py:27
  71.7 5.6 convert_bitcast_fusion
  77.3 11.4 %copy.11 = bf16[8,2048,256]{2,1,0:T(8,128)(2,1)} copy(bf16[8,2048,256]{1,2,0:T(8,128)(2,1)} %convert_bitcast_fusion) | data formatting | bytes 16777216 | tf_op jit(solution)/shard_map/while | solution.py:64
  88.7 333.1 %all-gather.8.cloned.1.call-done = bf16[32768,256]{1,0:T(8,128)(2,1)} async-done(((bf16[2048,256]{1,0:T(8,128)(2,1)}), bf16[32768,256]{1,0:T(8,128)(2,1)}) %all-gather.8.cloned.1.call-update) | async-done | bytes 16777232 | tf_op jit(solution)/shard_map/all_gather | solution.py:11
  421.8 9.9 reduce_sum.21
  431.7 6.8 convolution_convert_fusion
  441.5 79.0 %while.12 = (s32[]{:T(128)}, f32[8,256,256]{2,1,0:T(8,128)}, f32[8,256,256]{2,1,0:T(8,128)}, s32[]{:T(128)}, s32[32,3]{0,1:T(4,128)S(1)}, /*index=5*/s32[]{:T(12...) while((s32[]{:T(128)}, f32[8,256,256]{2,1,0:T(8,128)}, ...), condition=%wide.region_4.5_spmd, body=%wide.region_1.4_spmd.sunk | while | flops 808453248 | bytes 31462268 | solution.py:64
  441.6 4.0 gather_fusion
  445.6 1.8 gather_fusion.1
  448.2 2.7 select_convert_fusion.2
  450.8 5.0 gather_fusion.2
  455.8 2.0 fusion.30
  457.8 4.2 scatter_fusion
  463.8 4.3 scatter_fusion.1
  468.1 4.0 gather_fusion
  472.1 1.8 gather_fusion.1
  474.6 2.7 select_convert_fusion.2
  477.3 5.0 gather_fusion.2
  482.3 2.0 fusion.30
  484.3 4.1 scatter_fusion
  490.1 4.2 scatter_fusion.1
  494.5 4.0 gather_fusion
  498.5 1.8 gather_fusion.1
  501.0 2.7 select_convert_fusion.2
  503.7 5.0 gather_fusion.2
  508.6 2.0 fusion.30
  510.6 4.1 scatter_fusion
  516.5 4.1 scatter_fusion.1
  520.7 192.7 %all-reduce.2.cloned.1.call-done = f32[2048,256]{1,0:T(8,128)} async-done(((f32[2048,256]{1,0:T(8,128)}), f32[2048,256]{1,0:T(8,128)}) %all-reduce.2.cloned.1.call-update) | async-done | bytes 2097168 | tf_op jit(solution)/shard_map/psum | solution.py:67
  715.5 316.6 %all-gather.10.cloned.1.call-done = f32[32768,256]{1,0:T(8,128)} async-done(((f32[2048,256]{1,0:T(8,128)}), f32[32768,256]{1,0:T(8,128)}) %all-gather.10.cloned.1.call-update) | async-done | bytes 33554448 | tf_op jit(solution)/shard_map/all_gather | solution.py:11
  1032.2 12.3 %reduce_sum.22 = f32[2048,256]{1,0:T(8,128)S(1)} reduce(f32[16,2048,256]{2,1,0:T(8,128)} %bitcast.51, f32[]{:T(128)} %constant.59.clone.1), dimensions={0}, to_apply=%region_7.8 | reduce | flops 7864320 | bytes 35651588 | tf_op jit(solution)/shard_map/reduce_sum | solution.py:11
  1044.4 71.4 %reduce-scatter.2.cloned.1.call-done = f32[128,256]{1,0:T(8,128)} async-done(((f32[2048,256]{1,0:T(8,128)}), f32[128,256]{1,0:T(8,128)}) %reduce-scatter.2.cloned.1.call-update) | async-done | bytes 131088 | tf_op jit(solution)/shard_map/reduce_scatter | solution.py:68
  (40 shorter events, 16.0 us)
Async XLA Ops:
  6.5 65.1 %copy-start = (bf16[8,256,256]{2,1,0:T(8,128)(2,1)S(1)}, bf16[8,256,256]{2,1,0:T(8,128)(2,1)}, u32[]{:S(2)}) copy-start(bf16[8,256,256]{2,1,0:T(8,128)(2,1)} %param.8) | copy-start | bytes 3145732
  6.5 63.3 %all-gather.6.cloned.1.call-start = ((), (), s32[]{:S(2)}) async-start(), calls=%async_computation.1 | async-start | bytes 1114112 | tf_op jit(solution)/shard_map/all_gather | solution.py:27
  7.3 414.5 %all-gather.8.cloned.1.call-start = ((), (), s32[]{:S(2)}) async-start(), calls=%async_computation.4 | async-start | bytes 17825792 | tf_op jit(solution)/shard_map/all_gather | solution.py:11
  69.8 1.8 copy-start.2
  70.9 642.5 %all-reduce.2.cloned.1.call-start = ((), (), s32[]{:S(2)}) async-start(), calls=%async_computation.3 | async-start | bytes 4194304 | tf_op jit(solution)/shard_map/psum | solution.py:67
  438.5 3.0 copy-start.4
  520.6 511.6 %all-gather.10.cloned.1.call-start = ((), (), s32[]{:S(2)}) async-start(), calls=%async_computation.5 | async-start | bytes 35651584 | tf_op jit(solution)/shard_map/all_gather | solution.py:11
  714.9 400.9 %reduce-scatter.2.cloned.1.call-start = ((), (), s32[]{:S(2)}) async-start(), calls=%async_computation.2 | async-start | bytes 2228224 | tf_op jit(solution)/shard_map/reduce_scatter | solution.py:68
  1032.2 83.6 %copy-start.3 = (bf16[128,256]{1,0:T(8,128)(2,1)S(1)}, bf16[128,256]{1,0:T(8,128)(2,1)}, u32[]{:S(2)}) copy-start(bf16[128,256]{1,0:T(8,128)(2,1)} %param.7) | copy-start | bytes 196612
  1032.2 85.2 %copy-start.1 = (bf16[8,256,256]{2,1,0:T(8,128)(2,1)S(1)}, bf16[8,256,256]{2,1,0:T(8,128)(2,1)}, u32[]{:S(2)}) copy-start(bf16[8,256,256]{2,1,0:T(8,128)(2,1)} %param.8) | copy-start | bytes 3145732
Sparse Core Ops, SparseCore 0:
  10.1 59.7 all-gather.5
  71.6 350.0 all-gather.7
  520.7 192.6 all-reduce.1
  716.0 316.1 all-gather.9
  1036.3 79.5 reduce-scatter.1
